TPU v7x, 256 devices: a whole 4x4x8 slice. The times are simulated.
256 devices in a mesh: section: 16 (over y_hi, z), seq: 16 (over y_lo, x, core).
Axes of the slice: x: 4, y: 4 (y_hi: 2, y_lo: 2; y = y_hi * 2 + y_lo), z: 8, core: 2. Of those that a mesh axis runs over, the one named last changes fastest.
Arguments:
- stream: bfloat16 [16, 2048, 2048], P('section', 'seq'), may hold values from -6 to 6
- queries: bfloat16 [16, 2048, 2048], P('section', 'seq'), may hold values from -5 to 5
- key_rows: bfloat16 [16, 2048, 2048], P('section', 'seq'), may hold values from -5 to 5
- value_rows: bfloat16 [16, 2048, 2048], P('section', 'seq'), may hold values from -6 to 6
- o_weight: bfloat16 [16, 2048, 2048], P('section', 'seq'), may hold values from -0.125 to 0.125
- norm_gain: float32 [16, 2048], P('section'), may hold values from 0.1 to 1.9
- w_gate: bfloat16 [16, 2048, 7168], P('section', None, 'seq'), may hold values from -0.125 to 0.125
- w_up: bfloat16 [16, 2048, 7168], P('section', None, 'seq'), may hold values from -0.125 to 0.125
- w_down: bfloat16 [16, 7168, 2048], P('section', 'seq'), may hold values from -0.0625 to 0.0625
Outputs:
- passed: bfloat16 [16, 2048, 2048], P('section', 'seq')
All inputs are finite; a program needn't handle non-finite values.
Results may differ from a plain program's by a relative error of at most 0.012.
Values may be sent and summed in bfloat16 or wider, within the bound.
No kernel may reach another device: no remote copies, remote signals or barrier semaphores. Data moves between devices by JAX's collectives and lax.ppermute only.
A program may use at most 64 MiB of HBM per device.

v0:
```python
import jax
import jax.numpy as jnp
from jax import lax
from jax.sharding import PartitionSpec as P

HEADS = 16
HEAD_DIM = 128


def passed_along(block, axis, distance):
    devices = range(lax.axis_size(axis))
    route = [((i - distance) % len(devices), i) for i in devices]
    return lax.ppermute(block, axis, route)


def attend(queries, key_rows, value_rows):
    length = queries.shape[0]
    head_count = queries.shape[1]
    head_width = queries.shape[2]
    block = 512
    count = length // block
    query_blocks = queries.reshape(count, block, head_count, head_width)

    def one_block(pieces):
        block_index, query_block = pieces
        scores = jnp.einsum(
            "qhd,khd->hqk", query_block, key_rows, preferred_element_type=jnp.float32
        ) * head_width ** (-0.5)
        row_pos = lax.broadcasted_iota(jnp.int32, (block, length), 0) + block_index * block
        col_pos = lax.broadcasted_iota(jnp.int32, (block, length), 1)
        scores = jnp.where((col_pos <= row_pos)[None], scores, -1e30)
        highest = jnp.max(scores, axis=-1, keepdims=True)
        powers = jnp.exp(scores - highest)
        weights = (powers / jnp.sum(powers, axis=-1, keepdims=True)).astype(jnp.bfloat16)
        mixture = jnp.einsum(
            "hqk,khd->qhd", weights, value_rows, preferred_element_type=jnp.float32
        )
        return mixture.astype(jnp.bfloat16)

    mixed = lax.map(one_block, (jnp.arange(count, dtype=jnp.int32), query_blocks))
    return mixed.reshape(length, head_count, head_width)


def attend_heads(triple):
    length = triple[0].shape[0]
    group = triple[0].shape[2]
    width = triple[0].shape[3]
    flat = [piece.reshape(length, group, width) for piece in triple]
    mixed = attend(flat[0], flat[1], flat[2])
    return mixed.reshape(length, 1, group, width)


def shards(stream, queries, key_rows, value_rows, o_weight, norm_gain, w_gate, w_up, w_down):
    local_steps = stream.shape[1]
    model_width = stream.shape[2]
    groups = lax.axis_size("seq")
    group_heads = HEADS // groups
    block_rows = HEADS * HEAD_DIM // groups

    def split_heads(tensor):
        return tensor[0].reshape(local_steps, groups, group_heads, HEAD_DIM)

    attended = attend_heads(
        (
            lax.all_to_all(split_heads(queries), "seq", split_axis=1, concat_axis=0, tiled=True),
            lax.all_to_all(split_heads(key_rows), "seq", split_axis=1, concat_axis=0, tiled=True),
            lax.all_to_all(split_heads(value_rows), "seq", split_axis=1, concat_axis=0, tiled=True),
        )
    )
    returned = lax.all_to_all(attended, "seq", split_axis=0, concat_axis=1, tiled=True)
    flat_rows = returned.reshape(local_steps, HEADS * HEAD_DIM)
    piece = lax.all_gather(o_weight[0], "seq", axis=0, tiled=True)
    count = piece.shape[0] // block_rows
    columns = flat_rows.reshape(local_steps, count, block_rows)
    shaped = piece.reshape(count, block_rows, model_width)
    parts = jnp.einsum("tkb,kbd->ktd", columns, shaped, preferred_element_type=jnp.float32).astype(
        jnp.bfloat16
    )
    parts = lax.optimization_barrier(parts)
    projected = jnp.sum(parts.astype(jnp.float32), axis=0)
    residual = stream[0].astype(jnp.float32) + projected
    normed = (
        residual
        * lax.rsqrt(jnp.mean(residual * residual, axis=-1, keepdims=True) + 1e-05)
        * norm_gain[0]
    ).astype(jnp.bfloat16)
    gate_local = w_gate[0]
    up_local = w_up[0]
    down_local = w_down[0]
    piece = lax.all_gather(normed, "seq", axis=0, tiled=True)
    gate_pre = jnp.dot(piece, gate_local, preferred_element_type=jnp.float32)
    up_pre = jnp.dot(piece, up_local, preferred_element_type=jnp.float32)
    hidden = (jax.nn.silu(gate_pre) * up_pre).astype(jnp.bfloat16)
    partials = jnp.dot(hidden, down_local, preferred_element_type=jnp.float32)
    ffn_sum = lax.psum_scatter(
        partials.astype(jnp.bfloat16), "seq", scatter_dimension=0, tiled=True
    ).astype(jnp.float32)
    finished = (residual + ffn_sum).astype(jnp.bfloat16)
    passed = passed_along(finished, "section", 1)
    return passed[None]


def solution(mesh):
    placed = (
        P("section", "seq", None),
        P("section", "seq", None),
        P("section", "seq", None),
        P("section", "seq", None),
        P("section", "seq", None),
        P("section", None),
        P("section", None, "seq"),
        P("section", None, "seq"),
        P("section", "seq", None),
    )
    return jax.shard_map(
        shards, mesh=mesh, in_specs=placed, out_specs=P("section", "seq", None), check_vma=False
    )
```

profile of v0, /device:TPU:7, one launch (start us, length us, event | category | flops | bytes accessed | tf_op | source)
XLA Modules:
  0.0 287.4 jit_solution(17072727347162290342)
XLA Ops:
  6.5 0.7 all-gather.6.cloned.1.call-update
  7.3 2.0 copy.31
  9.3 6.1 %all-to-all-start = ((bf16[128,16,1,128]{0,3,2,1:T(8,128)(2,1)}), bf16[128,16,1,128]{0,3,2,1:T(8,128)(2,1)S(1)}, u32[]{:S(2)}, u32[]{:S(2)}) async-start(bf16[128,16,1,128]{0,3,2,1:T(8,128)(2,1)} %bitcast.10), calls=%async_computation | async-start | bytes 1048576 | tf_op jit(solution)/shard_map/all_to_all | solution.py:65
  15.4 2.1 copy.34
  17.5 6.4 %all-to-all-done = bf16[128,16,1,128]{0,3,2,1:T(8,128)(2,1)S(1)} async-done(((bf16[128,16,1,128]{0,3,2,1:T(8,128)(2,1)}), bf16[128,16,1,128]{0,3,2,1:T(8,128)(2,1)S(1)}, u32[]{:S(2)}, u32[]{:S(2)}) %all-to-all-start) | async-done | bytes 524320 | tf_op jit(solution)/shard_map/all_to_all | solution.py:65
  23.9 5.8 %all-to-all-start.1 = ((bf16[128,16,1,128]{0,3,2,1:T(8,128)(2,1)}), bf16[128,16,1,128]{0,3,2,1:T(8,128)(2,1)S(1)}, u32[]{:S(2)}, u32[]{:S(2)}) async-start(bf16[128,16,1,128]{0,3,2,1:T(8,128)(2,1)} %bitcast.16), calls=%async_computation.1 | async-start | bytes 1048576 | tf_op jit(solution)/shard_map/all_to_all | solution.py:66
  29.7 1.0 copy.37
  30.8 12.6 %all-to-all-done.1 = bf16[128,16,1,128]{0,3,2,1:T(8,128)(2,1)S(1)} async-done(((bf16[128,16,1,128]{0,3,2,1:T(8,128)(2,1)}), bf16[128,16,1,128]{0,3,2,1:T(8,128)(2,1)S(1)}, u32[]{:S(2)}, u32[]{:S(2)}) %all-to-all-start.1) | async-done | bytes 524320 | tf_op jit(solution)/shard_map/all_to_all | solution.py:66
  43.4 5.9 %all-to-all-start.2 = ((bf16[128,16,1,128]{0,3,2,1:T(8,128)(2,1)}), bf16[128,16,1,128]{0,3,2,1:T(8,128)(2,1)S(1)}, u32[]{:S(2)}, u32[]{:S(2)}) async-start(bf16[128,16,1,128]{0,3,2,1:T(8,128)(2,1)} %bitcast.21), calls=%async_computation.2 | async-start | bytes 1048576 | tf_op jit(solution)/shard_map/all_to_all | solution.py:67
  49.4 1.1 copy.33
  50.4 0.3 copy.36
  50.7 12.2 %all-to-all-done.2 = bf16[128,16,1,128]{0,3,2,1:T(8,128)(2,1)S(1)} async-done(((bf16[128,16,1,128]{0,3,2,1:T(8,128)(2,1)}), bf16[128,16,1,128]{0,3,2,1:T(8,128)(2,1)S(1)}, u32[]{:S(2)}, u32[]{:S(2)}) %all-to-all-start.2) | async-done | bytes 524320 | tf_op jit(solution)/shard_map/all_to_all | solution.py:67
  62.9 0.3 copy.39
  63.2 21.5 %while.10 = (s32[]{:T(128)}, bf16[4,512,1,128]{3,1,2,0:T(8,128)(2,1)}, s32[4]{0:T(128)S(1)}, bf16[4,512,1,128]{3,1,2,0:T(8,128)(2,1)}, bf16[2048,1,128]{2,0,1:T(...) while((s32[]{:T(128)}, bf16[4,512,1,128]{3,1,2,0:T(8,128)(2,1)}, ...), condition=%wide.region_3.4_spmd, body=%wide.region_0.3_spmd.sunk | while | flops 546373120 | bytes 13908097 | solution.py:40
  63.2 0.6 dynamic_slice.17
  64.5 1.9 fusion.25
  66.4 0.7 fusion.26
  67.1 1.5 fusion.27
  68.6 0.6 dynamic_slice.17
  69.9 1.9 fusion.25
  71.7 0.7 fusion.26
  72.5 1.5 fusion.27
  74.0 0.6 dynamic_slice.17
  75.2 1.9 fusion.25
  77.1 0.7 fusion.26
  77.8 1.5 fusion.27
  79.4 0.6 dynamic_slice.17
  80.6 1.9 fusion.25
  82.5 0.7 fusion.26
  83.2 1.5 fusion.27
  84.7 0.5 broadcast.27
  85.3 2.0 reduce.4
  87.5 14.2 %all_to_all.60 = bf16[16,2,8192]{2,1,0:T(2,128)(2,1)S(1)} all-to-all(bf16[16,2,8192]{2,1,0:T(2,128)(2,1)S(1)} %reshape.62), channel_id=1, replica_groups=mesh['section'=16,'seq'=16] {'seq'}, dimensions={0} | all-to-all | bytes 1048576 | tf_op jit(solution)/shard_map/all_to_all | solution.py:70
  101.7 0.5 reshape.63
  102.3 5.7 %convolution_convert_fusion.1 = bf16[16,128,2048]{2,1,0:T(8,128)(2,1)S(1)} fusion(bf16[128,16,128]{2,0,1:T(8,128)(2,1)S(1)} %bitcast.93, bf16[16,128,2048]{2,1,0:T(8,128)(2,1)} %bitcast.92), kind=kOutput, calls=%fused_computation.17 | convolution fusion | flops 1077936128 | bytes 17301504 | tf_op jit(solution)/shard_map/tkb,kbd->ktd/dot_general | solution.py:76
  108.1 1.8 convert_reduce_fusion
  109.9 0.2 multiply_reduce_fusion
  110.2 1.0 multiply_convert_fusion.1
  111.2 0.2 reduce-scatter.2.cloned.1.call-start
  111.4 56.7 %all-gather.4.cloned.1.call-done = bf16[2048,2048]{1,0:T(8,128)(2,1)} async-done(((bf16[128,2048]{1,0:T(8,128)(2,1)}), bf16[2048,2048]{1,0:T(8,128)(2,1)}) %all-gather.4.cloned.1.call-update) | async-done | bytes 8388624 | tf_op jit(solution)/shard_map/all_gather | solution.py:90
  168.1 7.2 %fusion.12 = f32[2048,448]{0,1:T(8,128)S(1)} fusion(bf16[2048,2048]{1,0:T(8,128)(2,1)} %all-gather.4.cloned.1.call-done, bf16[1,2048,448]{1,2,0:T(8,128)(2,1)} %param.17), kind=kOutput, calls=%fused_computation.21 | convolution fusion | flops 3758096384 | bytes 13893632 | tf_op jit(solution)/shard_map/dot_general | solution.py:91
  175.3 4.3 %multiply_convert_fusion = bf16[2048,448]{0,1:T(8,128)(2,1)S(1)} fusion(f32[2048,448]{0,1:T(8,128)S(1)} %fusion.12, bf16[2048,2048]{1,0:T(8,128)(2,1)S(1)} %copy-done.4, bf16[1,2048,448]{1,2,0:T(8,128)(2,1)S(1)} %copy-done.5), kind=kOutput, calls=%fused_computation.18 | convolution fusion | flops 3763601408 | bytes 15728640 | tf_op jit(solution)/shard_map/dot_general | solution.py:92
  179.6 6.9 %convolution_convert_fusion = bf16[2048,2048]{1,0:T(8,128)(2,1)} fusion(bf16[2048,448]{0,1:T(8,128)(2,1)S(1)} %multiply_convert_fusion, bf16[1,448,2048]{2,1,0:T(8,128)(2,1)S(1)} %copy-done), kind=kOutput, calls=%fused_computation.16 | convolution fusion | flops 3762290688 | bytes 12058624 | tf_op jit(solution)/shard_map/dot_general | solution.py:94
  186.5 76.5 %reduce-scatter.2.cloned.1.call-done = bf16[128,2048]{1,0:T(8,128)(2,1)} async-done(((bf16[2048,2048]{1,0:T(8,128)(2,1)}), bf16[128,2048]{1,0:T(8,128)(2,1)}) %reduce-scatter.2.cloned.1.call-update) | async-done | bytes 524304 | tf_op jit(solution)/shard_map/reduce_scatter | solution.py:95
  263.0 1.2 add_convert_fusion
  264.3 1.3 collective-permute-start
  265.6 14.5 %collective-permute-done = bf16[128,2048]{1,0:T(8,128)(2,1)S(1)} collective-permute-done((bf16[128,2048]{1,0:T(8,128)(2,1)S(1)}, bf16[128,2048]{1,0:T(8,128)(2,1)S(1)}, u32[]{:S(2)}, u32[]{:S(2)}) %collective-permute-start) | collective-permute-done | bytes 524320 | tf_op jit(solution)/shard_map/ppermute | solution.py:13
  280.1 0.8 copy.54
  (26 shorter events, 0.3 us)
Async XLA Ops:
  6.5 173.1 %copy-start = (bf16[1,448,2048]{2,1,0:T(8,128)(2,1)S(1)}, bf16[1,448,2048]{2,1,0:T(8,128)(2,1)}, u32[]{:S(2)}) copy-start(bf16[1,448,2048]{2,1,0:T(8,128)(2,1)} %param.19) | copy-start | bytes 5505028
  6.5 23.2 %copy-start.2 = (bf16[1,128,2048]{2,1,0:T(8,128)(2,1)S(1)}, bf16[1,128,2048]{2,1,0:T(8,128)(2,1)}, u32[]{:S(2)}) copy-start(bf16[1,128,2048]{2,1,0:T(8,128)(2,1)} %param.14) | copy-start | bytes 1572868
  6.5 95.8 %all-gather.6.cloned.1.call-start = ((), (), s32[]{:S(2)}) async-start(), calls=%async_computation.7 | async-start | bytes 8912896 | tf_op jit(solution)/shard_map/all_gather | solution.py:72
  9.3 14.6 %all-to-all-start = ((bf16[128,16,1,128]{0,3,2,1:T(8,128)(2,1)}), bf16[128,16,1,128]{0,3,2,1:T(8,128)(2,1)S(1)}, u32[]{:S(2)}, u32[]{:S(2)}) async-start(bf16[128,16,1,128]{0,3,2,1:T(8,128)(2,1)} %bitcast.10), calls=%async_computation | async-start | bytes 1048576 | tf_op jit(solution)/shard_map/all_to_all | solution.py:65
  23.9 19.5 %all-to-all-start.1 = ((bf16[128,16,1,128]{0,3,2,1:T(8,128)(2,1)}), bf16[128,16,1,128]{0,3,2,1:T(8,128)(2,1)S(1)}, u32[]{:S(2)}, u32[]{:S(2)}) async-start(bf16[128,16,1,128]{0,3,2,1:T(8,128)(2,1)} %bitcast.16), calls=%async_computation.1 | async-start | bytes 1048576 | tf_op jit(solution)/shard_map/all_to_all | solution.py:66
  43.4 19.6 %all-to-all-start.2 = ((bf16[128,16,1,128]{0,3,2,1:T(8,128)(2,1)}), bf16[128,16,1,128]{0,3,2,1:T(8,128)(2,1)S(1)}, u32[]{:S(2)}, u32[]{:S(2)}) async-start(bf16[128,16,1,128]{0,3,2,1:T(8,128)(2,1)} %bitcast.21), calls=%async_computation.2 | async-start | bytes 1048576 | tf_op jit(solution)/shard_map/all_to_all | solution.py:67
  49.3 118.8 %all-gather.4.cloned.1.call-start = ((), (), s32[]{:S(2)}) async-start(), calls=%async_computation.5 | async-start | bytes 8912896 | tf_op jit(solution)/shard_map/all_gather | solution.py:90
  108.0 1.9 copy-start.1
  108.1 2.1 copy-start.3
  111.2 151.9 %reduce-scatter.2.cloned.1.call-start = ((), (), s32[]{:S(2)}) async-start(), calls=%async_computation.6 | async-start | bytes 8912896 | tf_op jit(solution)/shard_map/reduce_scatter | solution.py:95
  168.1 7.2 %copy-start.4 = (bf16[2048,2048]{1,0:T(8,128)(2,1)S(1)}, bf16[2048,2048]{1,0:T(8,128)(2,1)}, u32[]{:S(2)}) copy-start(bf16[2048,2048]{1,0:T(8,128)(2,1)} %all-gather.4.cloned.1.call-done) | copy-start | bytes 25165828
  168.1 7.2 %copy-start.5 = (bf16[1,2048,448]{1,2,0:T(8,128)(2,1)S(1)}, bf16[1,2048,448]{1,2,0:T(8,128)(2,1)}, u32[]{:S(2)}) copy-start(bf16[1,2048,448]{1,2,0:T(8,128)(2,1)} %param.18) | copy-start | bytes 5505028
  264.3 15.8 %collective-permute-start = (bf16[128,2048]{1,0:T(8,128)(2,1)S(1)}, bf16[128,2048]{1,0:T(8,128)(2,1)S(1)}, u32[]{:S(2)}, u32[]{:S(2)}) collective-permute-start(bf16[128,2048]{1,0:T(8,128)(2,1)S(1)} %add_convert_fusion), channel_id=1, source_target_pairs={{240,0},{0,16},{16,32},{32,48},{48,64},{64,80},{80,96},{96,112},{1... | collective-permute-start | bytes 1572872 | tf_op jit(solution)/shard_map/ppermute | solution.py:13
Sparse Core Ops, SparseCore 0:
  9.2 69.0 all-gather.5
  111.3 56.7 all-gather.3
  186.6 76.3 reduce-scatter.1
where the time goes:
time: 288 us; the launch traced here: 287 us
  waiting for transfers between devices  180 us (62%)
  matrix products  37.7 us (13%)
  starting transfers between devices  19.4 us (7%)
  blocking collectives  14.2 us (5%)
  between operations  13.3 us (5%)
  local copies, waits for them, and re-layouts  11.3 us (4%)
  other arithmetic  9.18 us (3%)
    reduce_scatter x1, waiting for transfers between devices, shards(): lax.psum_scatter(partials.astype(jnp.bfloat16), 'seq', scatter_dimension=...  76.5 us
    all_gather x1, waiting for transfers between devices, shards(): piece = lax.all_gather(normed, 'seq', axis=0, tiled=True)  56.7 us
    ppermute x1, waiting for transfers between devices, passed_along(): return lax.ppermute(block, axis, route)  14.5 us
    all_to_all x1, blocking collectives, shards(): lax.all_to_all(attended, 'seq', split_axis=0, concat_axis=1, tiled=True)  14.2 us
    all_to_all x1, waiting for transfers between devices, shards(): lax.all_to_all(split_heads(key_rows), 'seq', split_axis=1, concat_axis=0,...  12.6 us
    all_to_all x1, waiting for transfers between devices, shards(): lax.all_to_all(split_heads(value_rows), 'seq', split_axis=1, concat_axis=...  12.2 us
    dot_general x4, matrix products, one_block(): jnp.einsum('qhd,khd->hqk', query_block, key_rows, preferred_element_type=...  7.47 us
    dot_general x1, matrix products, shards(): gate_pre = jnp.dot(piece, gate_local, preferred_element_type=jnp.float32)  7.2 us
  transfers between devices with their start and end apart: 7, of which 6 were waited for; matrix products, arithmetic and copies ran while one was open for 10% of the time, Pallas kernels for 0%

commit v1 on v0

--- a/solution.py
+++ b/solution.py
@@ -87,7 +87,9 @@
     gate_local = w_gate[0]
     up_local = w_up[0]
     down_local = w_down[0]
-    piece = lax.all_gather(normed, "seq", axis=0, tiled=True)
+    piece = jnp.concatenate(
+        lax.all_to_all(jnp.stack([normed] * lax.axis_size("seq")), "seq", 0, 0), axis=0
+    )
     gate_pre = jnp.dot(piece, gate_local, preferred_element_type=jnp.float32)
     up_pre = jnp.dot(piece, up_local, preferred_element_type=jnp.float32)
     hidden = (jax.nn.silu(gate_pre) * up_pre).astype(jnp.bfloat16)

time: 288 us -> 328 us (1.14)
  blocking collectives: 14.2 us -> 112 us
  waiting for transfers between devices: 180 us -> 124 us
    all_to_all x0 -> x1, blocking collectives: none -> 97.9 us  [shards(): lax.all_to_all(jnp.stack([normed] * lax.axis_size('seq')), 'seq', 0, 0)]
    all_gather x1 -> x0, waiting for transfers between devices: 56.7 us -> none  [shards(): piece = lax.all_gather(normed, 'seq', axis=0, tiled=True)]
  transfers between devices with their start and end apart: 7 -> 6, of which waited for: 6 -> 5; matrix products, arithmetic and copies ran while one was open for 10% -> 9% of each run, Pallas kernels for 0% -> 0%
where the time goes in v1:
time: 328 us; the launch traced here: 327 us
  waiting for transfers between devices  124 us (38%)
  blocking collectives  112 us (34%)
  matrix products  34.6 us (11%)
  starting transfers between devices  19.2 us (6%)
  between operations  13.6 us (4%)
  local copies, waits for them, and re-layouts  12.3 us (4%)
  other arithmetic  8.31 us (3%)
    all_to_all x1, blocking collectives, shards(): lax.all_to_all(jnp.stack([normed] * lax.axis_size('seq')), 'seq', 0, 0)  97.9 us
    reduce_scatter x1, waiting for transfers between devices, shards(): lax.psum_scatter(partials.astype(jnp.bfloat16), 'seq', scatter_dimension=...  77.8 us
    ppermute x1, waiting for transfers between devices, passed_along(): return lax.ppermute(block, axis, route)  14.5 us
    all_to_all x1, blocking collectives, shards(): lax.all_to_all(attended, 'seq', split_axis=0, concat_axis=1, tiled=True)  14.2 us
    all_to_all x1, waiting for transfers between devices, shards(): lax.all_to_all(split_heads(key_rows), 'seq', split_axis=1, concat_axis=0,...  12.6 us
    all_to_all x1, waiting for transfers between devices, shards(): lax.all_to_all(split_heads(value_rows), 'seq', split_axis=1, concat_axis=...  12.2 us
    dot_general x4, matrix products, one_block(): jnp.einsum('qhd,khd->hqk', query_block, key_rows, preferred_element_type=...  7.47 us
    dot_general x1, matrix products, shards(): partials = jnp.dot(hidden, down_local, preferred_element_type=jnp.float32)  6.92 us
  transfers between devices with their start and end apart: 6, of which 5 were waited for; matrix products, arithmetic and copies ran while one was open for 9% of the time, Pallas kernels for 0%

profile of v1, /device:TPU:7, one launch (start us, length us, event | category | flops | bytes accessed | tf_op | source)
XLA Modules:
  0.0 327.0 jit_solution(15948059061593022320)
XLA Ops:
  6.5 0.7 all-gather.3.cloned.1.call-update
  7.3 2.0 copy.31
  9.3 6.1 %all-to-all-start = ((bf16[128,16,1,128]{0,3,2,1:T(8,128)(2,1)}), bf16[128,16,1,128]{0,3,2,1:T(8,128)(2,1)S(1)}, u32[]{:S(2)}, u32[]{:S(2)}) async-start(bf16[128,16,1,128]{0,3,2,1:T(8,128)(2,1)} %bitcast.10), calls=%async_computation | async-start | bytes 1048576 | tf_op jit(solution)/shard_map/all_to_all | solution.py:65
  15.4 2.1 copy.34
  17.5 6.4 %all-to-all-done = bf16[128,16,1,128]{0,3,2,1:T(8,128)(2,1)S(1)} async-done(((bf16[128,16,1,128]{0,3,2,1:T(8,128)(2,1)}), bf16[128,16,1,128]{0,3,2,1:T(8,128)(2,1)S(1)}, u32[]{:S(2)}, u32[]{:S(2)}) %all-to-all-start) | async-done | bytes 524320 | tf_op jit(solution)/shard_map/all_to_all | solution.py:65
  23.9 5.8 %all-to-all-start.1 = ((bf16[128,16,1,128]{0,3,2,1:T(8,128)(2,1)}), bf16[128,16,1,128]{0,3,2,1:T(8,128)(2,1)S(1)}, u32[]{:S(2)}, u32[]{:S(2)}) async-start(bf16[128,16,1,128]{0,3,2,1:T(8,128)(2,1)} %bitcast.16), calls=%async_computation.1 | async-start | bytes 1048576 | tf_op jit(solution)/shard_map/all_to_all | solution.py:66
  29.7 1.1 copy.37
  30.8 12.6 %all-to-all-done.1 = bf16[128,16,1,128]{0,3,2,1:T(8,128)(2,1)S(1)} async-done(((bf16[128,16,1,128]{0,3,2,1:T(8,128)(2,1)}), bf16[128,16,1,128]{0,3,2,1:T(8,128)(2,1)S(1)}, u32[]{:S(2)}, u32[]{:S(2)}) %all-to-all-start.1) | async-done | bytes 524320 | tf_op jit(solution)/shard_map/all_to_all | solution.py:66
  43.4 5.9 %all-to-all-start.2 = ((bf16[128,16,1,128]{0,3,2,1:T(8,128)(2,1)}), bf16[128,16,1,128]{0,3,2,1:T(8,128)(2,1)S(1)}, u32[]{:S(2)}, u32[]{:S(2)}) async-start(bf16[128,16,1,128]{0,3,2,1:T(8,128)(2,1)} %bitcast.21), calls=%async_computation.2 | async-start | bytes 1048576 | tf_op jit(solution)/shard_map/all_to_all | solution.py:67
  49.4 1.0 copy.33
  50.4 0.3 copy.36
  50.7 12.2 %all-to-all-done.2 = bf16[128,16,1,128]{0,3,2,1:T(8,128)(2,1)S(1)} async-done(((bf16[128,16,1,128]{0,3,2,1:T(8,128)(2,1)}), bf16[128,16,1,128]{0,3,2,1:T(8,128)(2,1)S(1)}, u32[]{:S(2)}, u32[]{:S(2)}) %all-to-all-start.2) | async-done | bytes 524320 | tf_op jit(solution)/shard_map/all_to_all | solution.py:67
  62.9 0.3 copy.39
  63.2 21.5 %while.10 = (s32[]{:T(128)}, bf16[4,512,1,128]{3,1,2,0:T(8,128)(2,1)}, s32[4]{0:T(128)S(1)}, bf16[4,512,1,128]{3,1,2,0:T(8,128)(2,1)}, bf16[2048,1,128]{2,0,1:T(...) while((s32[]{:T(128)}, bf16[4,512,1,128]{3,1,2,0:T(8,128)(2,1)}, ...), condition=%wide.region_3.4_spmd, body=%wide.region_0.3_spmd.sunk | while | flops 546373120 | bytes 13908097 | solution.py:40
  63.2 0.6 dynamic_slice.17
  64.5 1.9 fusion.30
  66.4 0.7 fusion.31
  67.1 1.5 fusion.32
  68.6 0.6 dynamic_slice.17
  69.9 1.9 fusion.30
  71.7 0.7 fusion.31
  72.5 1.5 fusion.32
  74.0 0.6 dynamic_slice.17
  75.2 1.9 fusion.30
  77.1 0.7 fusion.31
  77.8 1.5 fusion.32
  79.4 0.6 dynamic_slice.17
  80.6 1.9 fusion.30
  82.5 0.7 fusion.31
  83.2 1.5 fusion.32
  84.7 0.5 broadcast.35
  85.2 2.0 reduce.4
  87.3 14.2 %all_to_all.65 = bf16[16,2,8192]{2,1,0:T(2,128)(2,1)S(1)} all-to-all(bf16[16,2,8192]{2,1,0:T(2,128)(2,1)S(1)} %reshape.81), channel_id=1, replica_groups=mesh['section'=16,'seq'=16] {'seq'}, dimensions={0} | all-to-all | bytes 1048576 | tf_op jit(solution)/shard_map/all_to_all | solution.py:70
  101.5 0.5 reshape.82
  102.2 5.7 %convolution_convert_fusion.1 = bf16[16,128,2048]{2,1,0:T(8,128)(2,1)S(1)} fusion(bf16[128,16,128]{2,0,1:T(8,128)(2,1)S(1)} %bitcast.101, bf16[16,128,2048]{2,1,0:T(8,128)(2,1)} %bitcast.98), kind=kOutput, calls=%fused_computation.17 | convolution fusion | flops 1077936128 | bytes 17301504 | tf_op jit(solution)/shard_map/tkb,kbd->ktd/dot_general | solution.py:76
  107.9 1.8 convert_reduce_fusion
  109.8 0.2 multiply_reduce_fusion
  110.0 0.2 fusion.18
  110.2 1.1 stack.5
  111.3 97.9 %all_to_all.66 = bf16[16,128,2048]{2,1,0:T(8,128)(2,1)S(1)} all-to-all(bf16[16,128,2048]{2,1,0:T(8,128)(2,1)S(1)} %stack.5), channel_id=1, replica_groups=mesh['section'=16,'seq'=16] {'seq'}, dimensions={0} | all-to-all | bytes 16777216 | tf_op jit(solution)/shard_map/all_to_all | solution.py:91
  209.2 4.0 %fusion.12 = f32[2048,448]{0,1:T(8,128)S(1)} fusion(bf16[2048,2048]{1,0:T(8,128)(2,1)S(1)} %bitcast.99, bf16[1,2048,448]{1,2,0:T(8,128)(2,1)S(1)} %copy-done.4), kind=kOutput, calls=%fused_computation.21 | convolution fusion | flops 3758096384 | bytes 13893632 | tf_op jit(solution)/shard_map/dot_general | solution.py:93
  213.2 4.3 %multiply_convert_fusion = bf16[2048,448]{0,1:T(8,128)(2,1)S(1)} fusion(f32[2048,448]{0,1:T(8,128)S(1)} %fusion.12, bf16[2048,2048]{1,0:T(8,128)(2,1)S(1)} %bitcast.100, bf16[1,2048,448]{1,2,0:T(8,128)(2,1)S(1)} %copy-done.5), kind=kOutput, calls=%fused_computation.18 | convolution fusion | flops 3763601408 | bytes 15728640 | tf_op jit(solution)/shard_map/dot_general | solution.py:94
  217.5 6.9 %convolution_convert_fusion = bf16[2048,2048]{1,0:T(8,128)(2,1)} fusion(bf16[2048,448]{0,1:T(8,128)(2,1)S(1)} %multiply_convert_fusion, bf16[1,448,2048]{2,1,0:T(8,128)(2,1)S(1)} %copy-done), kind=kOutput, calls=%fused_computation.16 | convolution fusion | flops 3762290688 | bytes 12058624 | tf_op jit(solution)/shard_map/dot_general | solution.py:96
  224.5 77.8 %reduce-scatter.2.cloned.1.call-done = bf16[128,2048]{1,0:T(8,128)(2,1)} async-done(((bf16[2048,2048]{1,0:T(8,128)(2,1)}), bf16[128,2048]{1,0:T(8,128)(2,1)}) %reduce-scatter.2.cloned.1.call-update) | async-done | bytes 524304 | tf_op jit(solution)/shard_map/reduce_scatter | solution.py:97
  302.3 1.2 add_convert_fusion
  303.5 1.4 collective-permute-start
  304.9 14.5 %collective-permute-done = bf16[128,2048]{1,0:T(8,128)(2,1)S(1)} collective-permute-done((bf16[128,2048]{1,0:T(8,128)(2,1)S(1)}, bf16[128,2048]{1,0:T(8,128)(2,1)S(1)}, u32[]{:S(2)}, u32[]{:S(2)}) %collective-permute-start) | collective-permute-done | bytes 524320 | tf_op jit(solution)/shard_map/ppermute | solution.py:13
  319.3 0.8 copy.54
  (25 shorter events, 0.3 us)
Async XLA Ops:
  6.5 211.0 %copy-start = (bf16[1,448,2048]{2,1,0:T(8,128)(2,1)S(1)}, bf16[1,448,2048]{2,1,0:T(8,128)(2,1)}, u32[]{:S(2)}) copy-start(bf16[1,448,2048]{2,1,0:T(8,128)(2,1)} %param.19) | copy-start | bytes 5505028
  6.5 23.2 %copy-start.2 = (bf16[1,128,2048]{2,1,0:T(8,128)(2,1)S(1)}, bf16[1,128,2048]{2,1,0:T(8,128)(2,1)}, u32[]{:S(2)}) copy-start(bf16[1,128,2048]{2,1,0:T(8,128)(2,1)} %param.14) | copy-start | bytes 1572868
  6.5 95.6 %all-gather.3.cloned.1.call-start = ((), (), s32[]{:S(2)}) async-start(), calls=%async_computation.7 | async-start | bytes 8912896 | tf_op jit(solution)/shard_map/all_gather | solution.py:72
  9.3 14.6 %all-to-all-start = ((bf16[128,16,1,128]{0,3,2,1:T(8,128)(2,1)}), bf16[128,16,1,128]{0,3,2,1:T(8,128)(2,1)S(1)}, u32[]{:S(2)}, u32[]{:S(2)}) async-start(bf16[128,16,1,128]{0,3,2,1:T(8,128)(2,1)} %bitcast.10), calls=%async_computation | async-start | bytes 1048576 | tf_op jit(solution)/shard_map/all_to_all | solution.py:65
  23.9 19.5 %all-to-all-start.1 = ((bf16[128,16,1,128]{0,3,2,1:T(8,128)(2,1)}), bf16[128,16,1,128]{0,3,2,1:T(8,128)(2,1)S(1)}, u32[]{:S(2)}, u32[]{:S(2)}) async-start(bf16[128,16,1,128]{0,3,2,1:T(8,128)(2,1)} %bitcast.16), calls=%async_computation.1 | async-start | bytes 1048576 | tf_op jit(solution)/shard_map/all_to_all | solution.py:66
  43.4 19.6 %all-to-all-start.2 = ((bf16[128,16,1,128]{0,3,2,1:T(8,128)(2,1)}), bf16[128,16,1,128]{0,3,2,1:T(8,128)(2,1)S(1)}, u32[]{:S(2)}, u32[]{:S(2)}) async-start(bf16[128,16,1,128]{0,3,2,1:T(8,128)(2,1)} %bitcast.21), calls=%async_computation.2 | async-start | bytes 1048576 | tf_op jit(solution)/shard_map/all_to_all | solution.py:67
  49.3 253.0 %reduce-scatter.2.cloned.1.call-start = ((), (), s32[]{:S(2)}) async-start(), calls=%async_computation.6 | async-start | bytes 8912896 | tf_op jit(solution)/shard_map/reduce_scatter | solution.py:97
  107.9 1.9 copy-start.1
  107.9 2.1 copy-start.3
  111.3 97.9 %copy-start.4 = (bf16[1,2048,448]{1,2,0:T(8,128)(2,1)S(1)}, bf16[1,2048,448]{1,2,0:T(8,128)(2,1)}, u32[]{:S(2)}) copy-start(bf16[1,2048,448]{1,2,0:T(8,128)(2,1)} %param.17) | copy-start | bytes 5505028
  209.2 4.0 %copy-start.5 = (bf16[1,2048,448]{1,2,0:T(8,128)(2,1)S(1)}, bf16[1,2048,448]{1,2,0:T(8,128)(2,1)}, u32[]{:S(2)}) copy-start(bf16[1,2048,448]{1,2,0:T(8,128)(2,1)} %param.18) | copy-start | bytes 5505028
  303.5 15.8 %collective-permute-start = (bf16[128,2048]{1,0:T(8,128)(2,1)S(1)}, bf16[128,2048]{1,0:T(8,128)(2,1)S(1)}, u32[]{:S(2)}, u32[]{:S(2)}) collective-permute-start(bf16[128,2048]{1,0:T(8,128)(2,1)S(1)} %add_convert_fusion), channel_id=1, source_target_pairs={{240,0},{0,16},{16,32},{32,48},{48,64},{64,80},{80,96},{96,112},{1... | collective-permute-start | bytes 1572872 | tf_op jit(solution)/shard_map/ppermute | solution.py:13
Sparse Core Ops, SparseCore 0:
  9.2 69.0 all-gather.2
  224.6 77.6 reduce-scatter.1
